TPU v7x, 32 devices: a whole 2x2x4 slice. The times are simulated.
32 devices in a mesh: groups: 1, ex: 16 (over z, y, core), layer: 2 (over x), pb: 1.
Axes of the slice: x: 2, y: 2, z: 4, core: 2. Of those that a mesh axis runs over, the one named last changes fastest.
Arguments:
- train_grads: float32 [2, 1536, 1024], P('layer', ('groups', 'ex')), may hold values from -64 to 64
- query_grads: float32 [2, 1, 512, 1024], P('layer', 'pb', ('groups', 'ex')), may hold values from -64 to 64
- damping: float32 [2], P('layer'), may hold values from 0.05 to 0.5
Outputs:
- influence: float32 [1536, 1, 512], P(('groups', 'ex'), 'pb', 'layer')
All inputs are finite; a program needn't handle non-finite values.
Results may differ from a plain program's by a relative error of at most 0.0003.
Values sent between devices are 32-bit elements; how exact they have to be, the bound alone decides.
A program may use at most 64 MiB of HBM per device.

v0:
```python
import jax
import jax.numpy as jnp
from jax import lax
from jax.sharding import PartitionSpec as P


def solve_rows(factor, rows_in):
    inner = lax.linalg.triangular_solve(
        factor, rows_in, left_side=False, lower=True, transpose_a=True
    )
    return lax.linalg.triangular_solve(
        factor, inner, left_side=False, lower=True, transpose_a=False
    )


def on_device(train_grads, query_grads, damping):
    layers_here, local_rows, coords = train_grads.shape
    total_rows = local_rows * lax.axis_size("ex")
    half_rows = local_rows // lax.axis_size("pb")
    own_rows = lax.dynamic_slice_in_dim(train_grads, lax.axis_index("pb") * half_rows, half_rows, 1)
    partial_gram = jnp.einsum("lnp,lnq->lpq", own_rows, own_rows, precision=lax.Precision.HIGHEST)
    gram_matrix = lax.psum(partial_gram, ("ex", "pb"))
    identity = jnp.eye(coords, dtype=jnp.float32)
    fisher = gram_matrix / total_rows + damping[:, None, None] * identity[None]
    factor = jnp.linalg.cholesky(fisher)
    queries = query_grads[:, 0]
    solved = solve_rows(factor, queries)
    score_tile = jnp.einsum(
        "lnp,lkp->nk",
        train_grads,
        lax.all_gather(solved, "ex", axis=1, tiled=True),
        precision=lax.Precision.HIGHEST,
    )
    shares = lax.psum_scatter(score_tile, "layer", scatter_dimension=1, tiled=True)
    return shares[:, None, :]


def solution(mesh):
    in_specs = (
        P("layer", ("groups", "ex"), None),
        P("layer", "pb", ("groups", "ex"), None),
        P("layer"),
    )
    out_specs = P(("groups", "ex"), "pb", "layer")
    return jax.shard_map(
        on_device, mesh=mesh, in_specs=in_specs, out_specs=out_specs, check_vma=False
    )
```

profile of v0, /device:TPU:0, one launch (start us, length us, event | category | flops | bytes accessed | tf_op | source)
XLA Modules:
  0.0 545.7 jit_solution(9678609055191033883)
XLA Ops:
  7.5 5.0 convolution_bitcast_fusion
  13.3 113.3 %all-reduce.3.cloned.1.call-done = f32[1,1024,1024]{1,2,0:T(8,128)} async-done(((f32[1,1024,1024]{1,2,0:T(8,128)}), f32[1,1024,1024]{1,2,0:T(8,128)}) %all-reduce.3.cloned.1.call-update) | async-done | bytes 4194320 | tf_op jit(solution)/shard_map/psum | solution.py:22
  126.6 5.1 select_add_fusion
  131.7 5.6 %copy.5 = f32[1,1024,1024]{2,1,0:T(8,128)} copy(f32[1,1024,1024]{1,2,0:T(8,128)} %select_add_fusion) | data formatting | bytes 8388608 | tf_op jit(solution)/shard_map/add | solution.py:24
  143.7 11.7 %custom-call.72 = f32[1,128,128]{2,1,0:T(8,128)S(1)} custom-call(f32[1,128,128]{2,1,0:T(8,128)S(1)} %cholesky.582), custom_call_target="Cholesky" | custom-call | tf_op jit(solution)/shard_map/jit(cholesky)/cholesky | solution.py:25
  155.6 9.8 %custom-call.73 = f32[1,1,128,128]{2,3,1,0:T(8,128)S(1)} custom-call(f32[1,1,128,128]{3,2,1,0:T(8,128)S(1)} %get-tuple-element.40), custom_call_target="InvertDiagBlocksLowerTriangular" | custom-call | tf_op jit(solution)/shard_map/jit(cholesky)/cholesky | solution.py:25
  168.7 11.7 %custom-call.74 = f32[1,128,128]{2,1,0:T(8,128)S(1)} custom-call(f32[1,128,128]{2,1,0:T(8,128)S(1)} %cholesky.586), custom_call_target="Cholesky" | custom-call | tf_op jit(solution)/shard_map/jit(cholesky)/cholesky | solution.py:25
  184.4 9.8 %custom-call.75 = f32[1,1,128,128]{2,3,1,0:T(8,128)S(1)} custom-call(f32[1,1,128,128]{3,2,1,0:T(8,128)S(1)} %get-tuple-element.38), custom_call_target="InvertDiagBlocksLowerTriangular" | custom-call | tf_op jit(solution)/shard_map/jit(cholesky)/cholesky | solution.py:25
  198.9 11.7 %custom-call.76 = f32[1,128,128]{2,1,0:T(8,128)S(1)} custom-call(f32[1,128,128]{2,1,0:T(8,128)S(1)} %cholesky.591), custom_call_target="Cholesky" | custom-call | tf_op jit(solution)/shard_map/jit(cholesky)/cholesky | solution.py:25
  211.3 9.8 %custom-call.77 = f32[1,1,128,128]{2,3,1,0:T(8,128)S(1)} custom-call(f32[1,1,128,128]{3,2,1,0:T(8,128)S(1)} %get-tuple-element.36), custom_call_target="InvertDiagBlocksLowerTriangular" | custom-call | tf_op jit(solution)/shard_map/jit(cholesky)/cholesky | solution.py:25
  225.7 11.7 %custom-call.78 = f32[1,128,128]{2,1,0:T(8,128)S(1)} custom-call(f32[1,128,128]{2,1,0:T(8,128)S(1)} %cholesky.596), custom_call_target="Cholesky" | custom-call | tf_op jit(solution)/shard_map/jit(cholesky)/cholesky | solution.py:25
  238.2 9.8 %custom-call.79 = f32[1,1,128,128]{2,3,1,0:T(8,128)S(1)} custom-call(f32[1,1,128,128]{3,2,1,0:T(8,128)S(1)} %get-tuple-element.34), custom_call_target="InvertDiagBlocksLowerTriangular" | custom-call | tf_op jit(solution)/shard_map/jit(cholesky)/cholesky | solution.py:25
  252.3 11.9 %custom-call.80 = f32[1,128,128]{2,1,0:T(8,128)S(1)} custom-call(f32[1,128,128]{2,1,0:T(8,128)S(1)} %cholesky.601), custom_call_target="Cholesky" | custom-call | tf_op jit(solution)/shard_map/jit(cholesky)/cholesky | solution.py:25
  265.0 9.8 %custom-call.81 = f32[1,1,128,128]{2,3,1,0:T(8,128)S(1)} custom-call(f32[1,1,128,128]{3,2,1,0:T(8,128)S(1)} %get-tuple-element.32), custom_call_target="InvertDiagBlocksLowerTriangular" | custom-call | tf_op jit(solution)/shard_map/jit(cholesky)/cholesky | solution.py:25
  279.0 11.7 %custom-call.82 = f32[1,128,128]{2,1,0:T(8,128)S(1)} custom-call(f32[1,128,128]{2,1,0:T(8,128)S(1)} %cholesky.606), custom_call_target="Cholesky" | custom-call | tf_op jit(solution)/shard_map/jit(cholesky)/cholesky | solution.py:25
  291.5 9.8 %custom-call.83 = f32[1,1,128,128]{2,3,1,0:T(8,128)S(1)} custom-call(f32[1,1,128,128]{3,2,1,0:T(8,128)S(1)} %get-tuple-element.30), custom_call_target="InvertDiagBlocksLowerTriangular" | custom-call | tf_op jit(solution)/shard_map/jit(cholesky)/cholesky | solution.py:25
  305.4 11.7 %custom-call.84 = f32[1,128,128]{2,1,0:T(8,128)S(1)} custom-call(f32[1,128,128]{2,1,0:T(8,128)S(1)} %cholesky.611), custom_call_target="Cholesky" | custom-call | tf_op jit(solution)/shard_map/jit(cholesky)/cholesky | solution.py:25
  317.9 9.8 %custom-call.85 = f32[1,1,128,128]{2,3,1,0:T(8,128)S(1)} custom-call(f32[1,1,128,128]{3,2,1,0:T(8,128)S(1)} %get-tuple-element.28), custom_call_target="InvertDiagBlocksLowerTriangular" | custom-call | tf_op jit(solution)/shard_map/jit(cholesky)/cholesky | solution.py:25
  330.7 11.7 %custom-call.86 = f32[1,128,128]{2,1,0:T(8,128)S(1)} custom-call(f32[1,128,128]{2,1,0:T(8,128)S(1)} %fusion.18), custom_call_target="Cholesky" | custom-call | tf_op jit(solution)/shard_map/jit(cholesky)/cholesky | solution.py:25
  352.9 4.9 select_select_fusion
  357.8 23.7 %while.1 = (s32[]{:T(128)}, f32[1,1024,1024]{1,2,0:T(8,128)}, s32[8,2]{0,1:T(2,128)S(1)}, f32[8,1,128,128]{3,2,1,0:T(8,128)S(1)}, s32[]{:T(128)}) while((s32[]{:T(128)}, f32[1,1024,1024]{1,2,0:T(8,128)}, s32[8,2]{0,1:T(2,128)S(1)}, f32[8,1,128,128]{3,2,1,0:T(8,128)S(1)}, s32[]{:T(128)}) %tuple.49), condition=%wide.while_cond, body=%wide.while_body.sunk | while | flops 2 | bytes 393333 | solution.py:8
  381.5 78.8 %custom-call.87 = f32[1,8,128,128]{2,3,1,0:T(8,128)S(1)} custom-call(f32[1,8,128,128]{3,2,1,0:T(8,128)S(1)} %bitcast.460), custom_call_target="InvertDiagBlocksLowerTriangular" | custom-call | tf_op jit(solution)/shard_map/triangular_solve | solution.py:8
  482.3 40.7 %all-gather.2.cloned.1.call-done = f32[1,512,1024]{2,1,0:T(8,128)} async-done(((f32[1,32,1024]{2,1,0:T(8,128)}), f32[1,512,1024]{2,1,0:T(8,128)}) %all-gather.2.cloned.1.call-update) | async-done | bytes 2097168 | tf_op jit(solution)/shard_map/all_gather | solution.py:31
  527.5 9.9 %reduce-scatter.2.cloned.1.call-done = f32[96,256]{1,0:T(8,128)} async-done(((f32[96,512]{1,0:T(8,128)}), f32[96,256]{1,0:T(8,128)}) %reduce-scatter.2.cloned.1.call-update) | async-done | bytes 98320 | tf_op jit(solution)/shard_map/reduce_scatter | solution.py:34
  (166 shorter events, 100.1 us)
Async XLA Ops:
  6.5 1.0 copy-start
  6.5 120.0 %all-reduce.3.cloned.1.call-start = ((), (), s32[]{:S(2)}) async-start(), calls=%async_computation.1 | async-start | bytes 8388608 | tf_op jit(solution)/shard_map/psum | solution.py:22
  12.6 510.4 %all-gather.2.cloned.1.call-start = ((), (), s32[]{:S(2)}) async-start(), calls=%async_computation.2 | async-start | bytes 2228224 | tf_op jit(solution)/shard_map/all_gather | solution.py:31
  141.8 1.9 copy-start.1
  352.9 107.4 %copy-start.3 = (f32[1,1,32,1024]{3,2,1,0:T(8,128)S(1)}, f32[1,1,32,1024]{3,2,1,0:T(8,128)}, u32[]{:S(2)}) copy-start(f32[1,1,32,1024]{3,2,1,0:T(8,128)} %param.4) | copy-start | bytes 393220
  481.6 0.7 copy-start.2
  482.3 55.1 %reduce-scatter.2.cloned.1.call-start = ((), (), s32[]{:S(2)}) async-start(), calls=%async_computation.3 | async-start | bytes 294912 | tf_op jit(solution)/shard_map/reduce_scatter | solution.py:34
Sparse Core Ops, SparseCore 0:
  12.7 113.8 all-reduce.2
  482.4 40.5 all-gather.1
  527.6 9.7 reduce-scatter.1
where the time goes:
time: 550 us; the launch traced here: 546 us
  other arithmetic  261 us (47%)
  waiting for transfers between devices  164 us (30%)
  matrix products  57.3 us (10%)
  local copies, waits for them, and re-layouts  43.8 us (8%)
  between operations  19.7 us (4%)
    another operation x30, other arithmetic, on_device(): factor = jnp.linalg.cholesky(fisher)  168 us
    psum x1, waiting for transfers between devices, on_device(): gram_matrix = lax.psum(partial_gram, ('ex', 'pb'))  113 us
    another operation x3, other arithmetic, solve_rows(): lax.linalg.triangular_solve(factor, rows_in, left_side=False, lower=True,...  83.6 us
    all_gather x1, waiting for transfers between devices, on_device(): lax.all_gather(solved, 'ex', axis=1, tiled=True)  40.7 us
    another operation x14, matrix products, on_device(): factor = jnp.linalg.cholesky(fisher)  27.2 us
    another operation x40, local copies, waits for them, and re-layouts  23.5 us
  transfers between devices with their start and end apart: 3, of which 3 were waited for; matrix products, arithmetic and copies ran while one was open for 0% of the time, Pallas kernels for 0%

commit v1 on v0

--- a/solution.py
+++ b/solution.py
@@ -2,6 +2,28 @@
 import jax.numpy as jnp
 from jax import lax
 from jax.sharding import PartitionSpec as P
+
+
+def joined_along(blocks, dim):
+    blocks = jnp.moveaxis(blocks, 0, dim)
+    lengths = blocks.shape
+    return blocks.reshape(*lengths[:dim], lengths[dim] * lengths[dim + 1], *lengths[dim + 2 :])
+
+
+def doubled(x, axis):
+    size = lax.axis_size(axis)
+    parts = x[None]
+    for level in range(size.bit_length() - 1):
+        stride = 1 << level
+        other = lax.ppermute(parts, axis, [(i, i ^ stride) for i in range(size)])
+        both = jnp.stack([parts, other])
+        upper = lax.axis_index(axis) >> level & 1
+        parts = jnp.where(upper == 0, both, both[::-1]).reshape(-1, *x.shape)
+    return parts
+
+
+def collect(shard, axis, dim):
+    return joined_along(doubled(shard, axis), dim)
 
 
 def solve_rows(factor, rows_in):
@@ -26,10 +48,7 @@
     queries = query_grads[:, 0]
     solved = solve_rows(factor, queries)
     score_tile = jnp.einsum(
-        "lnp,lkp->nk",
-        train_grads,
-        lax.all_gather(solved, "ex", axis=1, tiled=True),
-        precision=lax.Precision.HIGHEST,
+        "lnp,lkp->nk", train_grads, collect(solved, "ex", 1), precision=lax.Precision.HIGHEST
     )
     shares = lax.psum_scatter(score_tile, "layer", scatter_dimension=1, tiled=True)
     return shares[:, None, :]

time: 550 us -> 578 us (1.051)
  waiting for transfers between devices: 164 us -> 189 us
    ppermute x0 -> x4, waiting for transfers between devices: none -> 65.7 us  [doubled(): other = lax.ppermute(parts, axis, [(i, i ^ stride) for i in range(size)])]
    all_gather x1 -> x0, waiting for transfers between devices: 40.7 us -> none  [on_device(): lax.all_gather(solved, 'ex', axis=1, tiled=True)]
  transfers between devices with their start and end apart: 3 -> 6, of which waited for: 3 -> 6; matrix products, arithmetic and copies ran while one was open for 0% -> 0% of each run, Pallas kernels for 0% -> 0%
where the time goes in v1:
time: 578 us; the launch traced here: 574 us
  other arithmetic  262 us (45%)
  waiting for transfers between devices  189 us (33%)
  matrix products  55.5 us (10%)
  local copies, waits for them, and re-layouts  42.9 us (7%)
  between operations  20.1 us (3%)
    another operation x30, other arithmetic, on_device(): factor = jnp.linalg.cholesky(fisher)  168 us
    psum x1, waiting for transfers between devices, on_device(): gram_matrix = lax.psum(partial_gram, ('ex', 'pb'))  113 us
    another operation x3, other arithmetic, solve_rows(): lax.linalg.triangular_solve(factor, rows_in, left_side=False, lower=True,...  83.7 us
    ppermute x4, waiting for transfers between devices, doubled(): other = lax.ppermute(parts, axis, [(i, i ^ stride) for i in range(size)])  65.7 us
    another operation x14, matrix products, on_device(): factor = jnp.linalg.cholesky(fisher)  27 us
    another operation x40, local copies, waits for them, and re-layouts  23.5 us
  transfers between devices with their start and end apart: 6, of which 6 were waited for; matrix products, arithmetic and copies ran while one was open for 0% of the time, Pallas kernels for 0%

profile of v1, /device:TPU:0, one launch (start us, length us, event | category | flops | bytes accessed | tf_op | source)
XLA Modules:
  0.0 574.2 jit_solution(7146137266213412554)
XLA Ops:
  13.3 113.3 %all-reduce.3.cloned.1.call-done = f32[1,1024,1024]{1,2,0:T(8,128)} async-done(((f32[1,1024,1024]{1,2,0:T(8,128)}), f32[1,1024,1024]{1,2,0:T(8,128)}) %all-reduce.3.cloned.1.call-update) | async-done | bytes 4194320 | tf_op jit(solution)/shard_map/psum | solution.py:44
  126.6 5.1 select_add_fusion
  131.7 5.8 %copy.5 = f32[1,1024,1024]{2,1,0:T(8,128)} copy(f32[1,1024,1024]{1,2,0:T(8,128)} %select_add_fusion) | data formatting | bytes 8388608 | tf_op jit(solution)/shard_map/add | solution.py:46
  143.9 11.7 %custom-call.72 = f32[1,128,128]{2,1,0:T(8,128)S(1)} custom-call(f32[1,128,128]{2,1,0:T(8,128)S(1)} %cholesky.582), custom_call_target="Cholesky" | custom-call | tf_op jit(solution)/shard_map/jit(cholesky)/cholesky | solution.py:47
  155.8 9.8 %custom-call.73 = f32[1,1,128,128]{2,3,1,0:T(8,128)S(1)} custom-call(f32[1,1,128,128]{3,2,1,0:T(8,128)S(1)} %get-tuple-element.42), custom_call_target="InvertDiagBlocksLowerTriangular" | custom-call | tf_op jit(solution)/shard_map/jit(cholesky)/cholesky | solution.py:47
  168.9 11.7 %custom-call.74 = f32[1,128,128]{2,1,0:T(8,128)S(1)} custom-call(f32[1,128,128]{2,1,0:T(8,128)S(1)} %cholesky.586), custom_call_target="Cholesky" | custom-call | tf_op jit(solution)/shard_map/jit(cholesky)/cholesky | solution.py:47
  184.2 9.8 %custom-call.75 = f32[1,1,128,128]{2,3,1,0:T(8,128)S(1)} custom-call(f32[1,1,128,128]{3,2,1,0:T(8,128)S(1)} %get-tuple-element.40), custom_call_target="InvertDiagBlocksLowerTriangular" | custom-call | tf_op jit(solution)/shard_map/jit(cholesky)/cholesky | solution.py:47
  198.7 11.7 %custom-call.76 = f32[1,128,128]{2,1,0:T(8,128)S(1)} custom-call(f32[1,128,128]{2,1,0:T(8,128)S(1)} %cholesky.591), custom_call_target="Cholesky" | custom-call | tf_op jit(solution)/shard_map/jit(cholesky)/cholesky | solution.py:47
  211.2 9.8 %custom-call.77 = f32[1,1,128,128]{2,3,1,0:T(8,128)S(1)} custom-call(f32[1,1,128,128]{3,2,1,0:T(8,128)S(1)} %get-tuple-element.38), custom_call_target="InvertDiagBlocksLowerTriangular" | custom-call | tf_op jit(solution)/shard_map/jit(cholesky)/cholesky | solution.py:47
  225.6 11.7 %custom-call.78 = f32[1,128,128]{2,1,0:T(8,128)S(1)} custom-call(f32[1,128,128]{2,1,0:T(8,128)S(1)} %cholesky.596), custom_call_target="Cholesky" | custom-call | tf_op jit(solution)/shard_map/jit(cholesky)/cholesky | solution.py:47
  238.1 9.8 %custom-call.79 = f32[1,1,128,128]{2,3,1,0:T(8,128)S(1)} custom-call(f32[1,1,128,128]{3,2,1,0:T(8,128)S(1)} %get-tuple-element.36), custom_call_target="InvertDiagBlocksLowerTriangular" | custom-call | tf_op jit(solution)/shard_map/jit(cholesky)/cholesky | solution.py:47
  252.2 12.1 %custom-call.80 = f32[1,128,128]{2,1,0:T(8,128)S(1)} custom-call(f32[1,128,128]{2,1,0:T(8,128)S(1)} %cholesky.601), custom_call_target="Cholesky" | custom-call | tf_op jit(solution)/shard_map/jit(cholesky)/cholesky | solution.py:47
  265.0 9.8 %custom-call.81 = f32[1,1,128,128]{2,3,1,0:T(8,128)S(1)} custom-call(f32[1,1,128,128]{3,2,1,0:T(8,128)S(1)} %get-tuple-element.34), custom_call_target="InvertDiagBlocksLowerTriangular" | custom-call | tf_op jit(solution)/shard_map/jit(cholesky)/cholesky | solution.py:47
  279.1 11.7 %custom-call.82 = f32[1,128,128]{2,1,0:T(8,128)S(1)} custom-call(f32[1,128,128]{2,1,0:T(8,128)S(1)} %cholesky.606), custom_call_target="Cholesky" | custom-call | tf_op jit(solution)/shard_map/jit(cholesky)/cholesky | solution.py:47
  291.6 9.8 %custom-call.83 = f32[1,1,128,128]{2,3,1,0:T(8,128)S(1)} custom-call(f32[1,1,128,128]{3,2,1,0:T(8,128)S(1)} %get-tuple-element.32), custom_call_target="InvertDiagBlocksLowerTriangular" | custom-call | tf_op jit(solution)/shard_map/jit(cholesky)/cholesky | solution.py:47
  305.2 11.7 %custom-call.84 = f32[1,128,128]{2,1,0:T(8,128)S(1)} custom-call(f32[1,128,128]{2,1,0:T(8,128)S(1)} %cholesky.611), custom_call_target="Cholesky" | custom-call | tf_op jit(solution)/shard_map/jit(cholesky)/cholesky | solution.py:47
  317.7 9.8 %custom-call.85 = f32[1,1,128,128]{2,3,1,0:T(8,128)S(1)} custom-call(f32[1,1,128,128]{3,2,1,0:T(8,128)S(1)} %get-tuple-element.30), custom_call_target="InvertDiagBlocksLowerTriangular" | custom-call | tf_op jit(solution)/shard_map/jit(cholesky)/cholesky | solution.py:47
  330.5 11.7 %custom-call.86 = f32[1,128,128]{2,1,0:T(8,128)S(1)} custom-call(f32[1,128,128]{2,1,0:T(8,128)S(1)} %fusion.13), custom_call_target="Cholesky" | custom-call | tf_op jit(solution)/shard_map/jit(cholesky)/cholesky | solution.py:47
  357.6 23.7 %while.1 = (s32[]{:T(128)}, f32[1,1024,1024]{1,2,0:T(8,128)}, s32[8,2]{0,1:T(2,128)S(1)}, f32[8,1,128,128]{3,2,1,0:T(8,128)S(1)}, s32[]{:T(128)}) while((s32[]{:T(128)}, f32[1,1024,1024]{1,2,0:T(8,128)}, s32[8,2]{0,1:T(2,128)S(1)}, f32[8,1,128,128]{3,2,1,0:T(8,128)S(1)}, s32[]{:T(128)}) %tuple.50), condition=%wide.while_cond, body=%wide.while_body.sunk | while | flops 2 | bytes 393333 | solution.py:30
  381.4 78.8 %custom-call.87 = f32[1,8,128,128]{2,3,1,0:T(8,128)S(1)} custom-call(f32[1,8,128,128]{3,2,1,0:T(8,128)S(1)} %bitcast.482), custom_call_target="InvertDiagBlocksLowerTriangular" | custom-call | tf_op jit(solution)/shard_map/triangular_solve | solution.py:30
  484.2 7.2 %collective-permute-done.1 = f32[2,1,32,1024]{3,2,0,1:T(8,128)S(1)} collective-permute-done((f32[2,1,32,1024]{3,2,0,1:T(8,128)S(1)}, f32[2,1,32,1024]{3,2,0,1:T(8,128)S(1)}, u32[]{:S(2)}, u32[]{:S(2)}) %collective-permute-start.1) | collective-permute-done | bytes 262176 | tf_op jit(solution)/shard_map/ppermute | solution.py:18
  492.8 11.9 %collective-permute-done.2 = f32[4,1,32,1024]{3,2,0,1:T(8,128)S(1)} collective-permute-done((f32[4,1,32,1024]{3,2,0,1:T(8,128)S(1)}, f32[4,1,32,1024]{3,2,0,1:T(8,128)S(1)}, u32[]{:S(2)}, u32[]{:S(2)}) %collective-permute-start.2) | collective-permute-done | bytes 524320 | tf_op jit(solution)/shard_map/ppermute | solution.py:18
  506.5 45.3 %collective-permute-done.3 = f32[8,1,32,1024]{3,2,0,1:T(8,128)S(1)} collective-permute-done((f32[8,1,32,1024]{3,2,0,1:T(8,128)S(1)}, f32[8,1,32,1024]{3,2,0,1:T(8,128)S(1)}, u32[]{:S(2)}, u32[]{:S(2)}) %collective-permute-start.3) | collective-permute-done | bytes 1048608 | tf_op jit(solution)/shard_map/ppermute | solution.py:18
  555.2 10.3 %reduce-scatter.2.cloned.1.call-done = f32[96,256]{1,0:T(8,128)} async-done(((f32[96,512]{1,0:T(8,128)}), f32[96,256]{1,0:T(8,128)}) %reduce-scatter.2.cloned.1.call-update) | async-done | bytes 98320 | tf_op jit(solution)/shard_map/reduce_scatter | solution.py:53
  (177 shorter events, 113.5 us)
Async XLA Ops:
  6.5 1.0 copy-start
  6.5 120.0 %all-reduce.3.cloned.1.call-start = ((), (), s32[]{:S(2)}) async-start(), calls=%async_computation.1 | async-start | bytes 8388608 | tf_op jit(solution)/shard_map/psum | solution.py:44
  12.6 552.9 %reduce-scatter.2.cloned.1.call-start = ((), (), s32[]{:S(2)}) async-start(), calls=%async_computation.2 | async-start | bytes 294912 | tf_op jit(solution)/shard_map/reduce_scatter | solution.py:53
  142.0 1.9 copy-start.1
  352.7 107.4 %copy-start.2 = (f32[1,1,32,1024]{3,2,1,0:T(8,128)S(1)}, f32[1,1,32,1024]{3,2,1,0:T(8,128)}, u32[]{:S(2)}) copy-start(f32[1,1,32,1024]{3,2,1,0:T(8,128)} %param.4) | copy-start | bytes 393220
  481.5 1.4 collective-permute-start
  483.0 8.4 %collective-permute-start.1 = (f32[2,1,32,1024]{3,2,0,1:T(8,128)S(1)}, f32[2,1,32,1024]{3,2,0,1:T(8,128)S(1)}, u32[]{:S(2)}, u32[]{:S(2)}) collective-permute-start(f32[2,1,32,1024]{3,2,0,1:T(8,128)S(1)} %get-tuple-element.28), channel_id=1, source_target_pairs={{0,4},{2,6},{4,0},{6,2},{8,12},{10,14},{12,8},{14,10},{16,20},{18,... | collective-permute-start | bytes 786440 | tf_op jit(solution)/shard_map/ppermute | solution.py:18
  491.5 13.2 %collective-permute-start.2 = (f32[4,1,32,1024]{3,2,0,1:T(8,128)S(1)}, f32[4,1,32,1024]{3,2,0,1:T(8,128)S(1)}, u32[]{:S(2)}, u32[]{:S(2)}) collective-permute-start(f32[4,1,32,1024]{3,2,0,1:T(8,128)S(1)} %bitcast.453), channel_id=1, source_target_pairs={{0,8},{2,10},{4,12},{6,14},{8,0},{10,2},{12,4},{14,6},{16,24},{18,... | collective-permute-start | bytes 1572872 | tf_op jit(solution)/shard_map/ppermute | solution.py:18
  504.8 46.9 %collective-permute-start.3 = (f32[8,1,32,1024]{3,2,0,1:T(8,128)S(1)}, f32[8,1,32,1024]{3,2,0,1:T(8,128)S(1)}, u32[]{:S(2)}, u32[]{:S(2)}) collective-permute-start(f32[8,1,32,1024]{3,2,0,1:T(8,128)S(1)} %bitcast.450), channel_id=1, source_target_pairs={{0,16},{2,18},{4,20},{6,22},{8,24},{10,26},{12,28},{14,30},{16,0},... | collective-permute-start | bytes 3145736 | tf_op jit(solution)/shard_map/ppermute | solution.py:18
Sparse Core Ops, SparseCore 0:
  12.7 113.8 all-reduce.2
  555.3 10.1 reduce-scatter.1
